TPU v7x, 32 devices: a whole 2x2x4 slice. The times are simulated.
32 devices in a mesh: rep: 4 (over y, core), shard: 4 (over z), ctx: 2 (over x).
Axes of the slice: x: 2, y: 2, z: 4, core: 2. Of those that a mesh axis runs over, the one named last changes fastest.
Arguments:
- tokens: bfloat16 [2, 4, 512, 2048], P(None, 'rep', ('shard', 'ctx')), may hold values from -6 to 6
- span_starts: int32 [2, 4], P(None, 'rep'), may hold values from 0 to 256
- cotangent: bfloat16 [2, 4, 512, 2048], P(None, 'rep', ('shard', 'ctx')), may hold values from -6 to 6
- w_query: bfloat16 [2048, 2048], P('shard'), may hold values from -0.125 to 0.125
- key_weight: bfloat16 [2048, 1024], P('shard'), may hold values from -0.125 to 0.125
- value_weight: bfloat16 [2048, 1024], P('shard'), may hold values from -0.125 to 0.125
- w_out: bfloat16 [2048, 2048], P('shard'), may hold values from -0.75 to 0.75
- attn_gain: bfloat16 [2048], P('shard'), may hold values from 0.099609375 to 1.8984375
- query_gain: bfloat16 [128], P('shard'), may hold values from 0.099609375 to 1.8984375
- key_gain: bfloat16 [128], P('shard'), may hold values from 0.099609375 to 1.8984375
- w_gate: bfloat16 [2048, 6144], P('shard'), may hold values from -0.125 to 0.125
- w_up: bfloat16 [2048, 6144], P('shard'), may hold values from -0.125 to 0.125
- w_down: bfloat16 [6144, 2048], P('shard'), may hold values from -0.078125 to 0.078125
- ffn_gain: bfloat16 [2048], P('shard'), may hold values from 0.099609375 to 1.8984375
Outputs:
- output: bfloat16 [2, 4, 512, 2048], P(None, 'rep', ('shard', 'ctx'))
- input_grad: float32 [2, 4, 512, 2048], P(None, 'rep', ('shard', 'ctx'))
- grad_query: float32 [2048, 2048], P('shard')
- grad_key: float32 [2048, 1024], P('shard')
- grad_value: float32 [2048, 1024], P('shard')
- grad_out: float32 [2048, 2048], P('shard')
- grad_attn_gain: float32 [2048], P('shard')
- grad_query_gain: float32 [128], P('shard')
- grad_key_gain: float32 [128], P('shard')
- grad_gate: float32 [2048, 6144], P('shard')
- grad_up: float32 [2048, 6144], P('shard')
- grad_down: float32 [6144, 2048], P('shard')
- grad_ffn_gain: float32 [2048], P('shard')
Inputs may be any that keep to these rules, and one draw needn't show every extreme that they name: `span_starts`: each sequence's picture span covers positions start to start + 255 of that sequence.
All inputs are finite; a program needn't handle non-finite values.
Results may differ from a plain program's by a relative error of at most 0.023.
Values may be sent and summed in bfloat16 or wider, within the bound.
No kernel may reach another device: no remote copies, remote signals or barrier semaphores. Data moves between devices by JAX's collectives and lax.ppermute only.
A program may use at most 448 MiB of HBM per device.

v0:
```python
from functools import partial
import jax
import jax.numpy as jnp
from jax import lax
from jax.sharding import PartitionSpec as P

QUERY_HEADS = 16
KEY_VALUE_HEADS = 8
HEAD_SIZE = 128
PIC = 256
EPSILON = 1e-06
THETA = 1000000.0


def apply_rotation(values):
    half_width = values.shape[-1] // 2
    return jnp.concatenate([-values[..., half_width:], values[..., :half_width]], axis=-1)


def rotate_back(values):
    half_width = values.shape[-1] // 2
    return jnp.concatenate([values[..., half_width:], -values[..., :half_width]], axis=-1)


def spin_tables(positions):
    inverse = THETA ** (-jnp.arange(HEAD_SIZE // 2, dtype=jnp.float32) * 2.0 / HEAD_SIZE)
    angles = positions.astype(jnp.float32)[:, None] * inverse[None, :]
    cosine_table = jnp.concatenate([jnp.cos(angles), jnp.cos(angles)], axis=-1)[:, None, :]
    sine_values = jnp.concatenate([jnp.sin(angles), jnp.sin(angles)], axis=-1)[:, None, :]
    return (cosine_table, sine_values)


def recip_rms(values):
    return lax.rsqrt(jnp.mean(values * values, axis=-1, keepdims=True) + EPSILON)


def norm_back(unit, recip, gain, d_normed):
    d_unit = d_normed * gain
    return recip * (d_unit - unit * jnp.mean(d_unit * unit, axis=-1, keepdims=True))


def over_rows(left, right):
    return lax.dot_general(
        left, right, (((0,), (0,)), ((), ())), preferred_element_type=jnp.float32
    )


def compared_to(left, right):
    return lax.dot_general(
        left, right, (((1,), (1,)), ((), ())), preferred_element_type=jnp.float32
    )


def attention_set(w_query, key_weight, value_weight, w_out, attn_gain, query_gain, key_gain):
    return (
        lax.all_gather(w_query, "shard", axis=0, tiled=True),
        lax.all_gather(key_weight, "shard", axis=0, tiled=True),
        lax.all_gather(value_weight, "shard", axis=0, tiled=True),
        lax.all_gather(w_out, "shard", axis=0, tiled=True),
        lax.all_gather(attn_gain, "shard", axis=0, tiled=True),
        lax.all_gather(query_gain, "shard", axis=0, tiled=True),
        lax.all_gather(key_gain, "shard", axis=0, tiled=True),
    )


def feedforward_set(w_gate, w_up, w_down, ffn_gain):
    return (
        lax.all_gather(w_gate, "shard", axis=0, tiled=True),
        lax.all_gather(w_up, "shard", axis=0, tiled=True),
        lax.all_gather(w_down, "shard", axis=0, tiled=True),
        lax.all_gather(ffn_gain, "shard", axis=0, tiled=True),
    )


def masked_scores(allowed, q_head, k_head):
    scores = jnp.einsum(
        "tgd,sd->gts", q_head, k_head, preferred_element_type=jnp.float32
    ) * HEAD_SIZE ** (-0.5)
    return jnp.where(allowed, scores, -1e30)


def head_forward(allowed, pieces):
    q_head, k_head, v_head = pieces
    scores = masked_scores(allowed, q_head, k_head)
    highest = jnp.max(scores, axis=-1, keepdims=True)
    log_total = highest + jnp.log(jnp.sum(jnp.exp(scores - highest), axis=-1, keepdims=True))
    probs_low = jnp.exp(scores - log_total).astype(jnp.bfloat16)
    mixed = jnp.einsum("gts,sd->tgd", probs_low, v_head, preferred_element_type=jnp.float32)
    return (mixed, log_total)


def head_backward(allowed, pieces):
    q_head, k_head, v_head, d_mix_head, log_total = pieces
    probs = jnp.exp(masked_scores(allowed, q_head, k_head) - log_total)
    probs_low = probs.astype(jnp.bfloat16)
    d_probs = jnp.einsum("tgd,sd->gts", d_mix_head, v_head, preferred_element_type=jnp.float32)
    d_values = jnp.einsum("gts,tgd->sd", probs_low, d_mix_head, preferred_element_type=jnp.float32)
    row_dot = jnp.sum(probs * d_probs, axis=-1, keepdims=True)
    d_scores = (probs * (d_probs - row_dot)).astype(jnp.bfloat16)
    d_queries = jnp.einsum(
        "gts,sd->tgd", d_scores, k_head, preferred_element_type=jnp.float32
    ) * HEAD_SIZE ** (-0.5)
    d_keys = jnp.einsum(
        "gts,tgd->sd", d_scores, q_head, preferred_element_type=jnp.float32
    ) * HEAD_SIZE ** (-0.5)
    return (d_queries, d_keys, d_values)


def shards(
    tokens,
    span_starts,
    cotangent,
    w_query,
    key_weight,
    value_weight,
    w_out,
    attn_gain,
    query_gain,
    key_gain,
    w_gate,
    w_up,
    w_down,
    ffn_gain,
):
    seq_count = lax.axis_size(("shard", "ctx"))
    seq_rank = lax.axis_index(("shard", "ctx"))
    token_rows = tokens.shape[2]
    token_length = token_rows * seq_count
    group_width = QUERY_HEADS // KEY_VALUE_HEADS
    local_pos = seq_rank * token_rows + jnp.arange(token_rows, dtype=jnp.int32)
    key_pos = jnp.arange(token_length, dtype=jnp.int32)
    cosine_table, sine_values = spin_tables(local_pos)
    cos_keys = cosine_table[:, 0, :][None]
    sin_keys = sine_values[:, 0, :][None]
    out_list = []
    grad_list = []
    stored = []
    totals = None
    for micro_index in range(tokens.shape[0]):
        span_start = span_starts[micro_index, 0]
        inside_q = (local_pos >= span_start) & (local_pos < span_start + PIC)
        inside_k = (key_pos >= span_start) & (key_pos < span_start + PIC)
        allowed = (key_pos[None, :] <= local_pos[:, None]) | inside_q[:, None] & inside_k[None, :]
        hidden_in = tokens[micro_index, 0].astype(jnp.float32)
        full_query, full_key, full_value, complete_output, gain_attn, gain_query, gain_key = (
            attention_set(w_query, key_weight, value_weight, w_out, attn_gain, query_gain, key_gain)
        )
        gain_attn = gain_attn.astype(jnp.float32)
        gain_query = gain_query.astype(jnp.float32)
        gain_key = gain_key.astype(jnp.float32)
        recip_h = recip_rms(hidden_in)
        unit_h = hidden_in * recip_h
        normalized_rows = (unit_h * gain_attn).astype(jnp.bfloat16)
        q_pre = jnp.dot(normalized_rows, full_query, preferred_element_type=jnp.float32).reshape(
            token_rows, QUERY_HEADS, HEAD_SIZE
        )
        key_before_rotation = jnp.transpose(
            jnp.dot(normalized_rows, full_key, preferred_element_type=jnp.float32).reshape(
                token_rows, KEY_VALUE_HEADS, HEAD_SIZE
            ),
            (1, 0, 2),
        )
        value_local = jnp.transpose(
            jnp.dot(normalized_rows, full_value, preferred_element_type=jnp.float32)
            .astype(jnp.bfloat16)
            .reshape(token_rows, KEY_VALUE_HEADS, HEAD_SIZE),
            (1, 0, 2),
        )
        recip_q = recip_rms(q_pre)
        unit_query = q_pre * recip_q
        recip_k = recip_rms(key_before_rotation)
        unit_k = key_before_rotation * recip_k
        scaled_q = unit_query * gain_query
        scaled_k = unit_k * gain_key
        query_rows = jnp.transpose(
            (scaled_q * cosine_table + apply_rotation(scaled_q) * sine_values)
            .astype(jnp.bfloat16)
            .reshape(token_rows, KEY_VALUE_HEADS, group_width, HEAD_SIZE),
            (1, 0, 2, 3),
        )
        key_local = (scaled_k * cos_keys + apply_rotation(scaled_k) * sin_keys).astype(jnp.bfloat16)
        key_rows, value_matrix = (
            lax.all_gather(key_local, ("shard", "ctx"), axis=1, tiled=True),
            lax.all_gather(value_local, ("shard", "ctx"), axis=1, tiled=True),
        )
        mixed_split, log_total = lax.map(
            partial(head_forward, allowed), (query_rows, key_rows, value_matrix)
        )
        mixed_heads = (
            jnp.transpose(mixed_split, (1, 0, 2, 3))
            .reshape(token_rows, QUERY_HEADS * HEAD_SIZE)
            .astype(jnp.bfloat16)
        )
        middle = hidden_in + jnp.dot(
            mixed_heads, complete_output, preferred_element_type=jnp.float32
        )
        full_gate, full_up, full_down, gain_ffn = feedforward_set(w_gate, w_up, w_down, ffn_gain)
        gain_ffn = gain_ffn.astype(jnp.float32)
        recip_m = recip_rms(middle)
        unit_m = middle * recip_m
        ffn_in = (unit_m * gain_ffn).astype(jnp.bfloat16)
        gate_pre = jnp.dot(ffn_in, full_gate, preferred_element_type=jnp.float32)
        up_pre = jnp.dot(ffn_in, full_up, preferred_element_type=jnp.float32)
        sigma = jax.nn.sigmoid(gate_pre)
        act_gate = gate_pre * sigma
        inner_act = (act_gate * up_pre).astype(jnp.bfloat16)
        result = middle + jnp.dot(inner_act, full_down, preferred_element_type=jnp.float32)
        out_list.append(result.astype(jnp.bfloat16))
        cot_rows = cotangent[micro_index, 0]
        cot_float = cot_rows.astype(jnp.float32)
        d_inner = compared_to(cot_rows, full_down)
        d_gate = (d_inner * up_pre * sigma * (1.0 + gate_pre * (1.0 - sigma))).astype(jnp.bfloat16)
        d_up = (d_inner * act_gate).astype(jnp.bfloat16)
        d_ffn_in = compared_to(d_gate, full_gate) + compared_to(d_up, full_up)
        ffn_gain_part = jnp.sum(d_ffn_in * unit_m, axis=0)
        d_middle = cot_float + norm_back(unit_m, recip_m, gain_ffn, d_ffn_in)
        branch_gradient = d_middle.astype(jnp.bfloat16)
        d_mixed = jnp.transpose(
            compared_to(branch_gradient, complete_output)
            .astype(jnp.bfloat16)
            .reshape(token_rows, KEY_VALUE_HEADS, group_width, HEAD_SIZE),
            (1, 0, 2, 3),
        )
        d_split_q, d_keys, d_values = lax.map(
            partial(head_backward, allowed),
            (query_rows, key_rows, value_matrix, d_mixed, log_total),
        )
        d_queries = jnp.transpose(d_split_q, (1, 0, 2, 3)).reshape(
            token_rows, QUERY_HEADS, HEAD_SIZE
        )
        d_key_local, d_value_local = (
            lax.psum_scatter(
                d_keys.astype(jnp.bfloat16), ("shard", "ctx"), scatter_dimension=1, tiled=True
            ).astype(jnp.float32),
            lax.psum_scatter(
                d_values.astype(jnp.bfloat16), ("shard", "ctx"), scatter_dimension=1, tiled=True
            ).astype(jnp.float32),
        )
        d_unit_q = d_queries * cosine_table + rotate_back(d_queries * sine_values)
        d_unit_k = d_key_local * cos_keys + rotate_back(d_key_local * sin_keys)
        query_gain_part = jnp.sum(d_unit_q * unit_query, axis=(0, 1))
        key_gain_part = jnp.sum(d_unit_k * unit_k, axis=(0, 1))
        d_q_pre = (
            norm_back(unit_query, recip_q, gain_query, d_unit_q)
            .astype(jnp.bfloat16)
            .reshape(token_rows, QUERY_HEADS * HEAD_SIZE)
        )
        d_k_pre = jnp.transpose(
            norm_back(unit_k, recip_k, gain_key, d_unit_k).astype(jnp.bfloat16), (1, 0, 2)
        ).reshape(token_rows, KEY_VALUE_HEADS * HEAD_SIZE)
        d_v_pre = jnp.transpose(d_value_local.astype(jnp.bfloat16), (1, 0, 2)).reshape(
            token_rows, KEY_VALUE_HEADS * HEAD_SIZE
        )
        d_normed = (
            compared_to(d_q_pre, full_query)
            + compared_to(d_k_pre, full_key)
            + compared_to(d_v_pre, full_value)
        )
        attn_gain_part = jnp.sum(d_normed * unit_h, axis=0)
        grad_list.append(d_middle + norm_back(unit_h, recip_h, gain_attn, d_normed))
        stored.append(
            (
                normalized_rows,
                d_q_pre,
                d_k_pre,
                d_v_pre,
                mixed_heads,
                branch_gradient,
                ffn_in,
                d_gate,
                d_up,
                inner_act,
                cot_rows,
            )
        )
        parts = (attn_gain_part, query_gain_part, key_gain_part, ffn_gain_part)
        if totals is None:
            totals = parts
        else:
            totals = tuple((older + newer for older, newer in zip(totals, parts)))
    joined = [
        jnp.concatenate([saved_set[member] for saved_set in stored], axis=0) for member in range(11)
    ]
    (
        normed_all,
        dq_all,
        dk_all,
        dv_all,
        mixed_all,
        branch_all,
        ffn_all,
        gate_all,
        up_all,
        inner_all,
        cot_all,
    ) = joined
    totals = (
        lax.psum_scatter(
            over_rows(normed_all, dq_all).astype(jnp.bfloat16),
            "shard",
            scatter_dimension=0,
            tiled=True,
        ).astype(jnp.float32),
        lax.psum_scatter(
            over_rows(normed_all, dk_all).astype(jnp.bfloat16),
            "shard",
            scatter_dimension=0,
            tiled=True,
        ).astype(jnp.float32),
        lax.psum_scatter(
            over_rows(normed_all, dv_all).astype(jnp.bfloat16),
            "shard",
            scatter_dimension=0,
            tiled=True,
        ).astype(jnp.float32),
        lax.psum_scatter(
            over_rows(mixed_all, branch_all).astype(jnp.bfloat16),
            "shard",
            scatter_dimension=0,
            tiled=True,
        ).astype(jnp.float32),
        lax.psum_scatter(
            totals[0].astype(jnp.bfloat16), "shard", scatter_dimension=0, tiled=True
        ).astype(jnp.float32),
        lax.psum_scatter(
            totals[1].astype(jnp.bfloat16), "shard", scatter_dimension=0, tiled=True
        ).astype(jnp.float32),
        lax.psum_scatter(
            totals[2].astype(jnp.bfloat16), "shard", scatter_dimension=0, tiled=True
        ).astype(jnp.float32),
        lax.psum_scatter(
            over_rows(ffn_all, gate_all).astype(jnp.bfloat16),
            "shard",
            scatter_dimension=0,
            tiled=True,
        ).astype(jnp.float32),
        lax.psum_scatter(
            over_rows(ffn_all, up_all).astype(jnp.bfloat16),
            "shard",
            scatter_dimension=0,
            tiled=True,
        ).astype(jnp.float32),
        lax.psum_scatter(
            over_rows(inner_all, cot_all).astype(jnp.bfloat16),
            "shard",
            scatter_dimension=0,
            tiled=True,
        ).astype(jnp.float32),
        lax.psum_scatter(
            totals[3].astype(jnp.bfloat16), "shard", scatter_dimension=0, tiled=True
        ).astype(jnp.float32),
    )
    summed = (
        lax.psum(totals[0].astype(jnp.bfloat16), ("rep", "ctx")).astype(jnp.float32),
        lax.psum(totals[1].astype(jnp.bfloat16), ("rep", "ctx")).astype(jnp.float32),
        lax.psum(totals[2].astype(jnp.bfloat16), ("rep", "ctx")).astype(jnp.float32),
        lax.psum(totals[3].astype(jnp.bfloat16), ("rep", "ctx")).astype(jnp.float32),
        lax.psum(totals[4].astype(jnp.bfloat16), ("rep", "ctx")).astype(jnp.float32),
        lax.psum(totals[5].astype(jnp.bfloat16), ("rep", "ctx")).astype(jnp.float32),
        lax.psum(totals[6].astype(jnp.bfloat16), ("rep", "ctx")).astype(jnp.float32),
        lax.psum(totals[7].astype(jnp.bfloat16), ("rep", "ctx")).astype(jnp.float32),
        lax.psum(totals[8].astype(jnp.bfloat16), ("rep", "ctx")).astype(jnp.float32),
        lax.psum(totals[9].astype(jnp.bfloat16), ("rep", "ctx")).astype(jnp.float32),
        lax.psum(totals[10].astype(jnp.bfloat16), ("rep", "ctx")).astype(jnp.float32),
    )
    output = jnp.stack(out_list)[:, None]
    input_grad = jnp.stack(grad_list)[:, None]
    return (
        output,
        input_grad,
        summed[0],
        summed[1],
        summed[2],
        summed[3],
        summed[4],
        summed[5],
        summed[6],
        summed[7],
        summed[8],
        summed[9],
        summed[10],
    )


def solution(mesh):
    in_specs = (
        P(None, "rep", ("shard", "ctx"), None),
        P(None, "rep"),
        P(None, "rep", ("shard", "ctx"), None),
        P("shard", None),
        P("shard", None),
        P("shard", None),
        P("shard", None),
        P("shard"),
        P("shard"),
        P("shard"),
        P("shard", None),
        P("shard", None),
        P("shard", None),
        P("shard"),
    )
    out_specs = (
        P(None, "rep", ("shard", "ctx"), None),
        P(None, "rep", ("shard", "ctx"), None),
        P("shard", None),
        P("shard", None),
        P("shard", None),
        P("shard", None),
        P("shard"),
        P("shard"),
        P("shard"),
        P("shard", None),
        P("shard", None),
        P("shard", None),
        P("shard"),
    )
    return jax.shard_map(shards, mesh=mesh, in_specs=in_specs, out_specs=out_specs, check_vma=False)
```

profile of v0, /device:TPU:0, one launch (start us, length us, event | category | flops | bytes accessed | tf_op | source)
XLA Modules:
  0.0 4428.3 jit_solution(448300715896860769)
XLA Ops:
  36.3 57.1 %all-gather.18.cloned.1.call-done = bf16[2048,1024]{1,0:T(8,128)(2,1)} async-done(((bf16[512,1024]{1,0:T(8,128)(2,1)}), bf16[2048,1024]{1,0:T(8,128)(2,1)}) %all-gather.18.cloned.1.call-update) | async-done | bytes 4194320 | tf_op jit(solution)/shard_map/all_gather | solution.py:57
  108.0 66.2 %all-gather.14.cloned.1.call-done = bf16[2048,1024]{1,0:T(8,128)(2,1)} async-done(((bf16[512,1024]{1,0:T(8,128)(2,1)}), bf16[2048,1024]{1,0:T(8,128)(2,1)}) %all-gather.14.cloned.1.call-update) | async-done | bytes 4194320 | tf_op jit(solution)/shard_map/all_gather | solution.py:58
  204.3 119.9 %all-gather.22.cloned.1.call-done = bf16[2048,2048]{1,0:T(8,128)(2,1)} async-done(((bf16[512,2048]{1,0:T(8,128)(2,1)}), bf16[2048,2048]{1,0:T(8,128)(2,1)}) %all-gather.22.cloned.1.call-update) | async-done | bytes 8388624 | tf_op jit(solution)/shard_map/all_gather | solution.py:56
  365.2 41.6 all-gather.16.cloned.1.call-done
  406.8 21.4 while.56
  429.4 19.0 all-gather.34.cloned.1.call-done
  448.4 41.7 all-gather.32.cloned.1.call-done
  490.2 21.6 while.57
  512.4 127.8 %all-gather.24.cloned.1.call-done = bf16[2048,2048]{1,0:T(8,128)(2,1)} async-done(((bf16[512,2048]{1,0:T(8,128)(2,1)}), bf16[2048,2048]{1,0:T(8,128)(2,1)}) %all-gather.24.cloned.1.call-update) | async-done | bytes 8388624 | tf_op jit(solution)/shard_map/all_gather | solution.py:59
  647.8 417.4 %all-gather.26.cloned.1.call-done = bf16[2048,6144]{1,0:T(8,128)(2,1)} async-done(((bf16[512,6144]{1,0:T(8,128)(2,1)}), bf16[2048,6144]{1,0:T(8,128)(2,1)}) %all-gather.26.cloned.1.call-update) | async-done | bytes 25165840 | tf_op jit(solution)/shard_map/all_gather | solution.py:68
  1078.3 411.7 %all-gather.28.cloned.1.call-done = bf16[2048,6144]{1,0:T(8,128)(2,1)} async-done(((bf16[512,6144]{1,0:T(8,128)(2,1)}), bf16[2048,6144]{1,0:T(8,128)(2,1)}) %all-gather.28.cloned.1.call-update) | async-done | bytes 25165840 | tf_op jit(solution)/shard_map/all_gather | solution.py:69
  1503.4 411.6 %all-gather.30.cloned.1.call-done = bf16[6144,2048]{1,0:T(8,128)(2,1)} async-done(((bf16[1536,2048]{1,0:T(8,128)(2,1)}), bf16[6144,2048]{1,0:T(8,128)(2,1)}) %all-gather.30.cloned.1.call-update) | async-done | bytes 25165840 | tf_op jit(solution)/shard_map/all_gather | solution.py:70
  2033.3 55.3 %while.59 = (s32[]{:T(128)}, f32[8,64,2,128]{3,1,2,0:T(8,128)S(1)}, bf16[8,512,128]{2,1,0:T(8,128)(2,1)}, bf16[8,512,128]{2,1,0:T(8,128)(2,1)}, bf16[8,512,128]{...) while((s32[]{:T(128)}, f32[8,64,2,128]{3,1,2,0:T(8,128)S(1)}, ...), condition=%wide.region_28.29_spmd.clone, body=%wide.region_26.28_spmd.clone.sunk | while | flops 84656000 | bytes 3154369 | solution.py:224
  2102.3 60.2 %while.58 = (s32[]{:T(128)}, f32[8,64,2,128]{3,1,2,0:T(8,128)}, bf16[8,512,128]{2,1,0:T(8,128)(2,1)}, bf16[8,512,128]{2,1,0:T(8,128)(2,1)}, bf16[8,512,128]{2,1,...) while((s32[]{:T(128)}, f32[8,64,2,128]{3,1,2,0:T(8,128)}, ...), condition=%wide.region_19.20_spmd.clone, body=%wide.region_17.19_spmd.clone.sunk | while | flops 84656000 | bytes 3154369 | solution.py:224
  2165.4 63.3 %reduce-scatter.14.cloned.1.call-done = bf16[8,64,128]{2,1,0:T(8,128)(2,1)} async-done(((bf16[8,512,128]{2,1,0:T(8,128)(2,1)}), bf16[8,64,128]{2,1,0:T(8,128)(2,1)}) %reduce-scatter.14.cloned.1.call-update) | async-done | bytes 131088 | tf_op jit(solution)/shard_map/reduce_scatter | solution.py:235
  2234.1 61.2 %reduce-scatter.16.cloned.1.call-done = bf16[8,64,128]{2,1,0:T(8,128)(2,1)} async-done(((bf16[8,512,128]{2,1,0:T(8,128)(2,1)}), bf16[8,64,128]{2,1,0:T(8,128)(2,1)}) %reduce-scatter.16.cloned.1.call-update) | async-done | bytes 131088 | tf_op jit(solution)/shard_map/reduce_scatter | solution.py:232
  2295.3 67.1 %reduce-scatter.12.cloned.1.call-done = bf16[8,64,128]{2,1,0:T(8,128)(2,1)} async-done(((bf16[8,512,128]{2,1,0:T(8,128)(2,1)}), bf16[8,64,128]{2,1,0:T(8,128)(2,1)}) %reduce-scatter.12.cloned.1.call-update) | async-done | bytes 131088 | tf_op jit(solution)/shard_map/reduce_scatter | solution.py:232
  2440.9 80.1 %reduce-scatter.22.cloned.1.call-done = bf16[512,1024]{1,0:T(8,128)(2,1)} async-done(((bf16[2048,1024]{1,0:T(8,128)(2,1)}), bf16[512,1024]{1,0:T(8,128)(2,1)}) %reduce-scatter.22.cloned.1.call-update) | async-done | bytes 1048592 | tf_op jit(solution)/shard_map/reduce_scatter | solution.py:304
  2521.0 147.8 %reduce-scatter.26.cloned.1.call-done = bf16[512,2048]{1,0:T(8,128)(2,1)} async-done(((bf16[2048,2048]{1,0:T(8,128)(2,1)}), bf16[512,2048]{1,0:T(8,128)(2,1)}) %reduce-scatter.26.cloned.1.call-update) | async-done | bytes 2097168 | tf_op jit(solution)/shard_map/reduce_scatter | solution.py:316
  2668.8 148.2 %reduce-scatter.20.cloned.1.call-done = bf16[512,2048]{1,0:T(8,128)(2,1)} async-done(((bf16[2048,2048]{1,0:T(8,128)(2,1)}), bf16[512,2048]{1,0:T(8,128)(2,1)}) %reduce-scatter.20.cloned.1.call-update) | async-done | bytes 2097168 | tf_op jit(solution)/shard_map/reduce_scatter | solution.py:298
  2816.9 417.4 %reduce-scatter.30.cloned.1.call-done = bf16[512,6144]{1,0:T(8,128)(2,1)} async-done(((bf16[2048,6144]{1,0:T(8,128)(2,1)}), bf16[512,6144]{1,0:T(8,128)(2,1)}) %reduce-scatter.30.cloned.1.call-update) | async-done | bytes 6291472 | tf_op jit(solution)/shard_map/reduce_scatter | solution.py:337
  3234.3 418.7 %reduce-scatter.28.cloned.1.call-done = bf16[512,6144]{1,0:T(8,128)(2,1)} async-done(((bf16[2048,6144]{1,0:T(8,128)(2,1)}), bf16[512,6144]{1,0:T(8,128)(2,1)}) %reduce-scatter.28.cloned.1.call-update) | async-done | bytes 6291472 | tf_op jit(solution)/shard_map/reduce_scatter | solution.py:331
  3653.0 418.6 %reduce-scatter.32.cloned.1.call-done = bf16[1536,2048]{1,0:T(8,128)(2,1)} async-done(((bf16[6144,2048]{1,0:T(8,128)(2,1)}), bf16[1536,2048]{1,0:T(8,128)(2,1)}) %reduce-scatter.32.cloned.1.call-update) | async-done | bytes 6291472 | tf_op jit(solution)/shard_map/reduce_scatter | solution.py:343
  4143.1 248.2 %all-reduce.12.cloned.1.call-done = (bf16[512,2048]{1,0:T(8,128)(2,1)}, bf16[512,1024]{1,0:T(8,128)(2,1)}, bf16[512,1024]{1,0:T(8,128)(2,1)}, bf16[512,2048]{1,0...) async-done(((bf16[512,2048]{1,0:T(8,128)(2,1)}, bf16[512,1024]{1,0:T(8,128)(2,1)}, bf16[512,1024]{1,0:T(8,128)(2,1)}, ...) | async-done | bytes 25165840 | tf_op jit(solution)/shard_map/psum | solution.py:354
  (625 shorter events, 623.5 us)
Async XLA Ops:
  7.2 86.1 %all-gather.18.cloned.1.call-start = ((), (), s32[]{:S(2)}) async-start(), calls=%async_computation.13 | async-start | bytes 5242880 | tf_op jit(solution)/shard_map/all_gather | solution.py:57
  8.0 166.3 %all-gather.14.cloned.1.call-start = ((), (), s32[]{:S(2)}) async-start(), calls=%async_computation.11 | async-start | bytes 5242880 | tf_op jit(solution)/shard_map/all_gather | solution.py:58
  8.7 315.4 %all-gather.22.cloned.1.call-start = ((), (), s32[]{:S(2)}) async-start(), calls=%async_computation.15 | async-start | bytes 10485760 | tf_op jit(solution)/shard_map/all_gather | solution.py:56
  9.5 355.8 %all-gather.20.cloned.1.call-start = ((), (), s32[]{:S(2)}) async-start(), calls=%async_computation.14 | async-start | bytes 1179648 | tf_op jit(solution)/shard_map/all_gather | solution.py:183
  36.0 2327.7 %copy-start.56 = (f32[64,128]{1,0:T(8,128)}, f32[64,128]{1,0:T(8,128)S(1)}, u32[]{:S(2)}) copy-start(f32[64,128]{1,0:T(8,128)S(1)} %get-tuple-element.559) | copy-start | bytes 98308
  107.7 299.1 %all-gather.16.cloned.1.call-start = ((), (), s32[]{:S(2)}) async-start(), calls=%async_computation.12 | async-start | bytes 1179648 | tf_op jit(solution)/shard_map/all_gather | solution.py:184
  178.0 270.4 %all-gather.34.cloned.1.call-start = ((), (), s32[]{:S(2)}) async-start(), calls=%async_computation.21 | async-start | bytes 1179648 | tf_op jit(solution)/shard_map/all_gather | solution.py:183
  178.6 311.6 %all-gather.32.cloned.1.call-start = ((), (), s32[]{:S(2)}) async-start(), calls=%async_computation.20 | async-start | bytes 1179648 | tf_op jit(solution)/shard_map/all_gather | solution.py:184
  182.4 457.7 %all-gather.24.cloned.1.call-start = ((), (), s32[]{:S(2)}) async-start(), calls=%async_computation.16 | async-start | bytes 10485760 | tf_op jit(solution)/shard_map/all_gather | solution.py:59
  183.2 882.0 %all-gather.26.cloned.1.call-start = ((), (), s32[]{:S(2)}) async-start(), calls=%async_computation.17 | async-start | bytes 31457280 | tf_op jit(solution)/shard_map/all_gather | solution.py:68
  183.9 1306.1 %all-gather.28.cloned.1.call-start = ((), (), s32[]{:S(2)}) async-start(), calls=%async_computation.18 | async-start | bytes 31457280 | tf_op jit(solution)/shard_map/all_gather | solution.py:69
  184.5 1730.5 %all-gather.30.cloned.1.call-start = ((), (), s32[]{:S(2)}) async-start(), calls=%async_computation.19 | async-start | bytes 31457280 | tf_op jit(solution)/shard_map/all_gather | solution.py:70
  185.3 1978.6 %reduce-scatter.18.cloned.1.call-start = ((), (), s32[]{:S(2)}) async-start(), calls=%async_computation.25 | async-start | bytes 1179648 | tf_op jit(solution)/shard_map/reduce_scatter | solution.py:235
  2099.2 129.5 %reduce-scatter.14.cloned.1.call-start = ((), (), s32[]{:S(2)}) async-start(), calls=%async_computation.23 | async-start | bytes 1179648 | tf_op jit(solution)/shard_map/reduce_scatter | solution.py:235
  2162.6 132.7 %reduce-scatter.16.cloned.1.call-start = ((), (), s32[]{:S(2)}) async-start(), calls=%async_computation.24 | async-start | bytes 1179648 | tf_op jit(solution)/shard_map/reduce_scatter | solution.py:232
  2163.2 199.2 %reduce-scatter.12.cloned.1.call-start = ((), (), s32[]{:S(2)}) async-start(), calls=%async_computation.22 | async-start | bytes 1179648 | tf_op jit(solution)/shard_map/reduce_scatter | solution.py:232
  2163.8 277.1 %reduce-scatter.24.cloned.1.call-start = ((), (), s32[]{:S(2)}) async-start(), calls=%async_computation.28 | async-start | bytes 5242880 | tf_op jit(solution)/shard_map/reduce_scatter | solution.py:310
  2233.9 287.1 %reduce-scatter.22.cloned.1.call-start = ((), (), s32[]{:S(2)}) async-start(), calls=%async_computation.27 | async-start | bytes 5242880 | tf_op jit(solution)/shard_map/reduce_scatter | solution.py:304
  2371.2 297.6 %reduce-scatter.26.cloned.1.call-start = ((), (), s32[]{:S(2)}) async-start(), calls=%async_computation.29 | async-start | bytes 10485760 | tf_op jit(solution)/shard_map/reduce_scatter | solution.py:316
  2379.0 437.9 %reduce-scatter.20.cloned.1.call-start = ((), (), s32[]{:S(2)}) async-start(), calls=%async_computation.26 | async-start | bytes 10485760 | tf_op jit(solution)/shard_map/reduce_scatter | solution.py:298
  2390.6 843.8 %reduce-scatter.30.cloned.1.call-start = ((), (), s32[]{:S(2)}) async-start(), calls=%async_computation.31 | async-start | bytes 31457280 | tf_op jit(solution)/shard_map/reduce_scatter | solution.py:337
  2404.0 1249.0 %reduce-scatter.28.cloned.1.call-start = ((), (), s32[]{:S(2)}) async-start(), calls=%async_computation.30 | async-start | bytes 31457280 | tf_op jit(solution)/shard_map/reduce_scatter | solution.py:331
  2418.1 1653.6 %reduce-scatter.32.cloned.1.call-start = ((), (), s32[]{:S(2)}) async-start(), calls=%async_computation.32 | async-start | bytes 31457280 | tf_op jit(solution)/shard_map/reduce_scatter | solution.py:343
  2432.3 1958.9 %all-reduce.12.cloned.1.call-start = ((), (), s32[]{:S(2)}) async-start(), calls=%async_computation.33 | async-start | bytes 50331648 | tf_op jit(solution)/shard_map/psum | solution.py:354
  (107 other events, 9973.1 us)
Sparse Core Ops, SparseCore 0:
  9.6 83.6 all-gather.17
  94.9 79.2 all-gather.13
  175.8 148.2 all-gather.21
  326.8 38.4 all-gather.19
  367.8 38.9 all-gather.15
  409.4 38.9 all-gather.33
  451.2 38.9 all-gather.31
  491.7 148.4 all-gather.23
  641.8 423.3 all-gather.25
  1066.6 423.3 all-gather.27
  1491.6 423.3 all-gather.29
  2099.3 62.1 reduce-scatter.17
  2165.9 62.7 reduce-scatter.13
  2232.5 62.7 reduce-scatter.15
  2299.5 62.8 reduce-scatter.11
  2365.1 75.7 reduce-scatter.23
  2443.7 77.2 reduce-scatter.21
  2523.8 144.9 reduce-scatter.25
  2671.7 145.1 reduce-scatter.19
  2819.2 415.1 reduce-scatter.29
  3236.8 416.1 reduce-scatter.27
  3655.4 416.1 reduce-scatter.31
  4077.4 313.7 all-reduce.11
where the time goes:
time: 4440 us; the launch traced here: 4430 us
  waiting for transfers between devices  3820 us (86%)
  matrix products  416 us (9%)
  blocking collectives  66 us (1%)
  other arithmetic  63.2 us (1%)
    reduce_scatter x1, waiting for transfers between devices, shards(): lax.psum_scatter(over_rows(ffn_all, gate_all).astype(jnp.bfloat16), 'shar...  419 us
    reduce_scatter x1, waiting for transfers between devices, shards(): lax.psum_scatter(over_rows(inner_all, cot_all).astype(jnp.bfloat16), 'sha...  419 us
    all_gather x1, waiting for transfers between devices, feedforward_set(): lax.all_gather(w_gate, 'shard', axis=0, tiled=True)  417 us
    reduce_scatter x1, waiting for transfers between devices, shards(): lax.psum_scatter(over_rows(ffn_all, up_all).astype(jnp.bfloat16), 'shard'...  417 us
    all_gather x1, waiting for transfers between devices, feedforward_set(): lax.all_gather(w_up, 'shard', axis=0, tiled=True)  412 us
    all_gather x1, waiting for transfers between devices, feedforward_set(): lax.all_gather(w_down, 'shard', axis=0, tiled=True)  412 us
    psum x1, waiting for transfers between devices, shards(): lax.psum(totals[0].astype(jnp.bfloat16), ('rep', 'ctx')).astype(jnp.float32)  248 us
    reduce_scatter x1, waiting for transfers between devices, shards(): lax.psum_scatter(over_rows(normed_all, dq_all).astype(jnp.bfloat16), 'sha...  148 us
  transfers between devices with their start and end apart: 23, of which 22 were waited for; matrix products, arithmetic and copies ran while one was open for 7% of the time, Pallas kernels for 0%

commit v1 on v0

--- a/solution.py
+++ b/solution.py
@@ -10,6 +10,25 @@
 PIC = 256
 EPSILON = 1e-06
 THETA = 1000000.0
+
+
+def leaves_spread(u_in, dim_at):
+    v_next = list(u_in.shape[1:])
+    v_next[dim_at] *= u_in.shape[0]
+    return jnp.moveaxis(u_in, 0, dim_at).reshape(v_next)
+
+
+def _guide_quarters(message, a_name):
+    z_new = jax.lax.axis_size(a_name)
+    high = jax.lax.axis_index(a_name)
+    mixed_arr, low = (z_new, high)
+    g_now, met_up = (message[None], 1)
+    while met_up < mixed_arr:
+        y = jax.lax.ppermute(g_now, a_name, [(d, d ^ met_up) for d in range(mixed_arr)])
+        earlier = low & met_up == 0
+        g_now = jnp.concatenate([jnp.where(earlier, g_now, y), jnp.where(earlier, y, g_now)])
+        met_up *= 2
+    return g_now
 
 
 def apply_rotation(values):
@@ -64,10 +83,15 @@
 
 
 def feedforward_set(w_gate, w_up, w_down, ffn_gain):
+
+    def part_slots(s0, vector, which_dim):
+        block_last = _guide_quarters(s0, vector)
+        return leaves_spread(block_last, which_dim)
+
     return (
         lax.all_gather(w_gate, "shard", axis=0, tiled=True),
         lax.all_gather(w_up, "shard", axis=0, tiled=True),
-        lax.all_gather(w_down, "shard", axis=0, tiled=True),
+        part_slots(w_down, "shard", 0),
         lax.all_gather(ffn_gain, "shard", axis=0, tiled=True),
     )
 

time: 4440 us -> 4690 us (1.056)
  blocking collectives: 66 us -> 331 us
  waiting for transfers between devices: 3820 us -> 3750 us
  other arithmetic: 63.2 us -> 112 us
    all_gather x1 -> x0, waiting for transfers between devices: 412 us -> none  [feedforward_set(): lax.all_gather(w_down, 'shard', axis=0, tiled=True)]
    all_gather x1, blocking collectives: 14.3 us -> 278 us  [feedforward_set(): lax.all_gather(ffn_gain, 'shard', axis=0, tiled=True)]
    all_gather x2, waiting for transfers between devices: 83.3 us -> 347 us  [shards(): lax.all_gather(value_local, ('shard', 'ctx'), axis=1, tiled=True)]
    all_gather x2, waiting for transfers between devices: 37 us -> 279 us  [shards(): lax.all_gather(key_local, ('shard', 'ctx'), axis=1, tiled=True)]
    all_gather x1, waiting for transfers between devices: 120 us -> 0.01 us  [attention_set(): lax.all_gather(w_query, 'shard', axis=0, tiled=True)]
  transfers between devices with their start and end apart: 23 -> 24, of which waited for: 22 -> 20; matrix products, arithmetic and copies ran while one was open for 7% -> 7% of each run, Pallas kernels for 0% -> 0%
where the time goes in v1:
time: 4690 us; the launch traced here: 4670 us
  waiting for transfers between devices  3750 us (80%)
  matrix products  409 us (9%)
  blocking collectives  331 us (7%)
  other arithmetic  112 us (2%)
  local copies, waits for them, and re-layouts  50.9 us (1%)
    reduce_scatter x1, waiting for transfers between devices, shards(): lax.psum_scatter(over_rows(ffn_all, gate_all).astype(jnp.bfloat16), 'shar...  419 us
    reduce_scatter x1, waiting for transfers between devices, shards(): lax.psum_scatter(over_rows(ffn_all, up_all).astype(jnp.bfloat16), 'shard'...  419 us
    reduce_scatter x1, waiting for transfers between devices, shards(): lax.psum_scatter(over_rows(inner_all, cot_all).astype(jnp.bfloat16), 'sha...  418 us
    all_gather x1, waiting for transfers between devices, feedforward_set(): lax.all_gather(w_up, 'shard', axis=0, tiled=True)  411 us
    all_gather x1, waiting for transfers between devices, feedforward_set(): lax.all_gather(w_gate, 'shard', axis=0, tiled=True)  378 us
    all_gather x2, waiting for transfers between devices, shards(): lax.all_gather(value_local, ('shard', 'ctx'), axis=1, tiled=True)  347 us
    all_gather x2, waiting for transfers between devices, shards(): lax.all_gather(key_local, ('shard', 'ctx'), axis=1, tiled=True)  279 us
    all_gather x1, blocking collectives, feedforward_set(): lax.all_gather(ffn_gain, 'shard', axis=0, tiled=True)  278 us
  transfers between devices with their start and end apart: 24, of which 20 were waited for; matrix products, arithmetic and copies ran while one was open for 7% of the time, Pallas kernels for 0%

profile of v1, /device:TPU:0, one launch (start us, length us, event | category | flops | bytes accessed | tf_op | source)
XLA Modules:
  0.0 4674.9 jit_solution(12912534979594036416)
XLA Ops:
  40.6 52.7 %all-gather.17.cloned.1.call-done = bf16[2048,1024]{1,0:T(8,128)(2,1)} async-done(((bf16[512,1024]{1,0:T(8,128)(2,1)}), bf16[2048,1024]{1,0:T(8,128)(2,1)}) %all-gather.17.cloned.1.call-update) | async-done | bytes 4194320 | tf_op jit(solution)/shard_map/all_gather | solution.py:76
  109.9 64.3 %all-gather.13.cloned.1.call-done = bf16[2048,1024]{1,0:T(8,128)(2,1)} async-done(((bf16[512,1024]{1,0:T(8,128)(2,1)}), bf16[2048,1024]{1,0:T(8,128)(2,1)}) %all-gather.13.cloned.1.call-update) | async-done | bytes 4194320 | tf_op jit(solution)/shard_map/all_gather | solution.py:77
  184.7 278.4 %all-gather.1 = bf16[4,1,512]{2,1,0:T(2,128)(2,1)S(1)} all-gather(bf16[1,1,512]{2,1,0:T(2,128)(2,1)S(1)} %reshape.361), channel_id=1, replica_groups=mesh['rep'=4,'shard'=4,'ctx'=2] {'shard'}, dimensions={0}, use_global_device_ids=true | all-gather | bytes 5120 | tf_op jit(solution)/shard_map/all_gather | solution.py:95
  505.4 259.9 %all-gather.19.cloned.1.call-done = bf16[8,512,128]{2,1,0:T(8,128)(2,1)} async-done(((bf16[8,64,128]{2,1,0:T(8,128)(2,1)}), bf16[8,512,128]{2,1,0:T(8,128)(2,1)}) %all-gather.19.cloned.1.call-update) | async-done | bytes 1048592 | tf_op jit(solution)/shard_map/all_gather | solution.py:207
  765.3 305.5 %all-gather.15.cloned.1.call-done = bf16[8,512,128]{2,1,0:T(8,128)(2,1)} async-done(((bf16[8,64,128]{2,1,0:T(8,128)(2,1)}), bf16[8,512,128]{2,1,0:T(8,128)(2,1)}) %all-gather.15.cloned.1.call-update) | async-done | bytes 1048592 | tf_op jit(solution)/shard_map/all_gather | solution.py:208
  1070.8 21.4 while.56
  1112.4 41.7 all-gather.29.cloned.1.call-done
  1154.2 21.6 while.57
  1176.4 127.7 %all-gather.23.cloned.1.call-done = bf16[2048,2048]{1,0:T(8,128)(2,1)} async-done(((bf16[512,2048]{1,0:T(8,128)(2,1)}), bf16[2048,2048]{1,0:T(8,128)(2,1)}) %all-gather.23.cloned.1.call-update) | async-done | bytes 8388624 | tf_op jit(solution)/shard_map/all_gather | solution.py:78
  1330.7 20.5 pad_maximum_fusion
  1351.2 378.0 %all-gather.25.cloned.1.call-done = bf16[2048,6144]{1,0:T(8,128)(2,1)} async-done(((bf16[512,6144]{1,0:T(8,128)(2,1)}), bf16[2048,6144]{1,0:T(8,128)(2,1)}) %all-gather.25.cloned.1.call-update) | async-done | bytes 25165840 | tf_op jit(solution)/shard_map/all_gather | solution.py:92
  1742.8 411.2 %all-gather.27.cloned.1.call-done = bf16[2048,6144]{1,0:T(8,128)(2,1)} async-done(((bf16[512,6144]{1,0:T(8,128)(2,1)}), bf16[2048,6144]{1,0:T(8,128)(2,1)}) %all-gather.27.cloned.1.call-update) | async-done | bytes 25165840 | tf_op jit(solution)/shard_map/all_gather | solution.py:93
  2285.8 50.2 %while.59 = (s32[]{:T(128)}, f32[8,64,2,128]{3,1,2,0:T(8,128)S(1)}, bf16[8,512,128]{2,1,0:T(8,128)(2,1)S(1)}, bf16[8,512,128]{2,1,0:T(8,128)(2,1)}, bf16[8,512,1...) while((s32[]{:T(128)}, f32[8,64,2,128]{3,1,2,0:T(8,128)S(1)}, ...), condition=%wide.region_28.29_spmd.clone, body=%wide.region_26.28_spmd.clone.sunk | while | flops 84656000 | bytes 3154369 | solution.py:248
  2347.6 60.5 %while.58 = (s32[]{:T(128)}, f32[8,64,2,128]{3,1,2,0:T(8,128)S(1)}, bf16[8,512,128]{2,1,0:T(8,128)(2,1)}, bf16[8,512,128]{2,1,0:T(8,128)(2,1)}, bf16[8,512,128]{...) while((s32[]{:T(128)}, f32[8,64,2,128]{3,1,2,0:T(8,128)S(1)}, ...), condition=%wide.region_19.20_spmd.clone, body=%wide.region_17.19_spmd.clone.sunk | while | flops 84656000 | bytes 3154369 | solution.py:248
  2410.5 64.2 %reduce-scatter.14.cloned.1.call-done = bf16[8,64,128]{2,1,0:T(8,128)(2,1)} async-done(((bf16[8,512,128]{2,1,0:T(8,128)(2,1)}), bf16[8,64,128]{2,1,0:T(8,128)(2,1)}) %reduce-scatter.14.cloned.1.call-update) | async-done | bytes 131088 | tf_op jit(solution)/shard_map/reduce_scatter | solution.py:259
  2479.1 62.4 %reduce-scatter.16.cloned.1.call-done = bf16[8,64,128]{2,1,0:T(8,128)(2,1)} async-done(((bf16[8,512,128]{2,1,0:T(8,128)(2,1)}), bf16[8,64,128]{2,1,0:T(8,128)(2,1)}) %reduce-scatter.16.cloned.1.call-update) | async-done | bytes 131088 | tf_op jit(solution)/shard_map/reduce_scatter | solution.py:256
  2541.5 67.1 %reduce-scatter.12.cloned.1.call-done = bf16[8,64,128]{2,1,0:T(8,128)(2,1)} async-done(((bf16[8,512,128]{2,1,0:T(8,128)(2,1)}), bf16[8,64,128]{2,1,0:T(8,128)(2,1)}) %reduce-scatter.12.cloned.1.call-update) | async-done | bytes 131088 | tf_op jit(solution)/shard_map/reduce_scatter | solution.py:256
  2687.1 80.1 %reduce-scatter.22.cloned.1.call-done = bf16[512,1024]{1,0:T(8,128)(2,1)} async-done(((bf16[2048,1024]{1,0:T(8,128)(2,1)}), bf16[512,1024]{1,0:T(8,128)(2,1)}) %reduce-scatter.22.cloned.1.call-update) | async-done | bytes 1048592 | tf_op jit(solution)/shard_map/reduce_scatter | solution.py:328
  2767.2 147.8 %reduce-scatter.26.cloned.1.call-done = bf16[512,2048]{1,0:T(8,128)(2,1)} async-done(((bf16[2048,2048]{1,0:T(8,128)(2,1)}), bf16[512,2048]{1,0:T(8,128)(2,1)}) %reduce-scatter.26.cloned.1.call-update) | async-done | bytes 2097168 | tf_op jit(solution)/shard_map/reduce_scatter | solution.py:340
  2915.0 148.0 %reduce-scatter.20.cloned.1.call-done = bf16[512,2048]{1,0:T(8,128)(2,1)} async-done(((bf16[2048,2048]{1,0:T(8,128)(2,1)}), bf16[512,2048]{1,0:T(8,128)(2,1)}) %reduce-scatter.20.cloned.1.call-update) | async-done | bytes 2097168 | tf_op jit(solution)/shard_map/reduce_scatter | solution.py:322
  3063.0 417.5 %reduce-scatter.32.cloned.1.call-done = bf16[1536,2048]{1,0:T(8,128)(2,1)} async-done(((bf16[6144,2048]{1,0:T(8,128)(2,1)}), bf16[1536,2048]{1,0:T(8,128)(2,1)}) %reduce-scatter.32.cloned.1.call-update) | async-done | bytes 6291472 | tf_op jit(solution)/shard_map/reduce_scatter | solution.py:367
  3480.5 418.5 %reduce-scatter.30.cloned.1.call-done = bf16[512,6144]{1,0:T(8,128)(2,1)} async-done(((bf16[2048,6144]{1,0:T(8,128)(2,1)}), bf16[512,6144]{1,0:T(8,128)(2,1)}) %reduce-scatter.30.cloned.1.call-update) | async-done | bytes 6291472 | tf_op jit(solution)/shard_map/reduce_scatter | solution.py:361
  3899.1 418.6 %reduce-scatter.28.cloned.1.call-done = bf16[512,6144]{1,0:T(8,128)(2,1)} async-done(((bf16[2048,6144]{1,0:T(8,128)(2,1)}), bf16[512,6144]{1,0:T(8,128)(2,1)}) %reduce-scatter.28.cloned.1.call-update) | async-done | bytes 6291472 | tf_op jit(solution)/shard_map/reduce_scatter | solution.py:355
  4389.2 248.1 %all-reduce.12.cloned.1.call-done = (bf16[512,2048]{1,0:T(8,128)(2,1)}, bf16[512,1024]{1,0:T(8,128)(2,1)}, bf16[512,1024]{1,0:T(8,128)(2,1)}, bf16[512,2048]{1,0...) async-done(((bf16[512,2048]{1,0:T(8,128)(2,1)}, bf16[512,1024]{1,0:T(8,128)(2,1)}, bf16[512,1024]{1,0:T(8,128)(2,1)}, ...) | async-done | bytes 25165840 | tf_op jit(solution)/shard_map/psum | solution.py:378
  (652 shorter events, 641.1 us)
Async XLA Ops:
  7.2 86.1 %all-gather.17.cloned.1.call-start = ((), (), s32[]{:S(2)}) async-start(), calls=%async_computation.13 | async-start | bytes 5242880 | tf_op jit(solution)/shard_map/all_gather | solution.py:76
  7.9 166.3 %all-gather.13.cloned.1.call-start = ((), (), s32[]{:S(2)}) async-start(), calls=%async_computation.11 | async-start | bytes 5242880 | tf_op jit(solution)/shard_map/all_gather | solution.py:77
  8.7 473.8 %all-gather.21.cloned.1.call-start = ((), (), s32[]{:S(2)}) async-start(), calls=%async_computation.15 | async-start | bytes 10485760 | tf_op jit(solution)/shard_map/all_gather | solution.py:75
  9.4 755.9 %all-gather.19.cloned.1.call-start = ((), (), s32[]{:S(2)}) async-start(), calls=%async_computation.14 | async-start | bytes 1179648 | tf_op jit(solution)/shard_map/all_gather | solution.py:207
  109.6 961.2 %all-gather.15.cloned.1.call-start = ((), (), s32[]{:S(2)}) async-start(), calls=%async_computation.12 | async-start | bytes 1179648 | tf_op jit(solution)/shard_map/all_gather | solution.py:208
  177.9 934.5 %all-gather.31.cloned.1.call-start = ((), (), s32[]{:S(2)}) async-start(), calls=%async_computation.20 | async-start | bytes 1179648 | tf_op jit(solution)/shard_map/all_gather | solution.py:207
  178.5 975.6 %all-gather.29.cloned.1.call-start = ((), (), s32[]{:S(2)}) async-start(), calls=%async_computation.19 | async-start | bytes 1179648 | tf_op jit(solution)/shard_map/all_gather | solution.py:208
  182.4 1121.8 %all-gather.23.cloned.1.call-start = ((), (), s32[]{:S(2)}) async-start(), calls=%async_computation.16 | async-start | bytes 10485760 | tf_op jit(solution)/shard_map/all_gather | solution.py:78
  183.1 1546.0 %all-gather.25.cloned.1.call-start = ((), (), s32[]{:S(2)}) async-start(), calls=%async_computation.17 | async-start | bytes 31457280 | tf_op jit(solution)/shard_map/all_gather | solution.py:92
  183.9 1970.1 %all-gather.27.cloned.1.call-start = ((), (), s32[]{:S(2)}) async-start(), calls=%async_computation.18 | async-start | bytes 31457280 | tf_op jit(solution)/shard_map/all_gather | solution.py:93
  184.5 2225.1 %reduce-scatter.18.cloned.1.call-start = ((), (), s32[]{:S(2)}) async-start(), calls=%async_computation.24 | async-start | bytes 1179648 | tf_op jit(solution)/shard_map/reduce_scatter | solution.py:259
  184.5 283.1 %collective-permute-start = (bf16[1,1536,2048]{2,1,0:T(8,128)(2,1)}, bf16[1,1536,2048]{2,1,0:T(8,128)(2,1)}, u32[]{:S(2)}, u32[]{:S(2)}) collective-permute-start(bf16[1,1536,2048]{2,1,0:T(8,128)(2,1)} %bitcast.558), channel_id=1, source_target_pairs={{0,2},{2,0},{4,6},{6,4},{1,3},{3,1},{5,7},{7,5},{8,10},{10,8},{12,... | collective-permute-start | bytes 18874376 | tf_op jit(solution)/shard_map/ppermute | solution.py:27
  481.5 830.3 %collective-permute-start.1 = (bf16[2,1536,2048]{2,1,0:T(8,128)(2,1)}, bf16[2,1536,2048]{2,1,0:T(8,128)(2,1)}, u32[]{:S(2)}, u32[]{:S(2)}) collective-permute-start(bf16[2,1536,2048]{2,1,0:T(8,128)(2,1)} %pad_maximum_fusion.1), channel_id=1, source_target_pairs={{0,4},{2,6},{4,0},{6,2},{1,5},{3,7},{5,1},{7,3},{8,12},{10,14},{12... | collective-permute-start | bytes 37748744 | tf_op jit(solution)/shard_map/ppermute | solution.py:27
  2345.2 129.5 %reduce-scatter.14.cloned.1.call-start = ((), (), s32[]{:S(2)}) async-start(), calls=%async_computation.22 | async-start | bytes 1179648 | tf_op jit(solution)/shard_map/reduce_scatter | solution.py:259
  2408.2 133.3 %reduce-scatter.16.cloned.1.call-start = ((), (), s32[]{:S(2)}) async-start(), calls=%async_computation.23 | async-start | bytes 1179648 | tf_op jit(solution)/shard_map/reduce_scatter | solution.py:256
  2408.9 199.7 %reduce-scatter.12.cloned.1.call-start = ((), (), s32[]{:S(2)}) async-start(), calls=%async_computation.21 | async-start | bytes 1179648 | tf_op jit(solution)/shard_map/reduce_scatter | solution.py:256
  2409.5 277.6 %reduce-scatter.24.cloned.1.call-start = ((), (), s32[]{:S(2)}) async-start(), calls=%async_computation.27 | async-start | bytes 5242880 | tf_op jit(solution)/shard_map/reduce_scatter | solution.py:334
  2479.1 288.2 %reduce-scatter.22.cloned.1.call-start = ((), (), s32[]{:S(2)}) async-start(), calls=%async_computation.26 | async-start | bytes 5242880 | tf_op jit(solution)/shard_map/reduce_scatter | solution.py:328
  2616.5 298.5 %reduce-scatter.26.cloned.1.call-start = ((), (), s32[]{:S(2)}) async-start(), calls=%async_computation.28 | async-start | bytes 10485760 | tf_op jit(solution)/shard_map/reduce_scatter | solution.py:340
  2622.6 440.4 %reduce-scatter.20.cloned.1.call-start = ((), (), s32[]{:S(2)}) async-start(), calls=%async_computation.25 | async-start | bytes 10485760 | tf_op jit(solution)/shard_map/reduce_scatter | solution.py:322
  2635.4 845.1 %reduce-scatter.32.cloned.1.call-start = ((), (), s32[]{:S(2)}) async-start(), calls=%async_computation.31 | async-start | bytes 31457280 | tf_op jit(solution)/shard_map/reduce_scatter | solution.py:367
  2650.4 1248.7 %reduce-scatter.30.cloned.1.call-start = ((), (), s32[]{:S(2)}) async-start(), calls=%async_computation.30 | async-start | bytes 31457280 | tf_op jit(solution)/shard_map/reduce_scatter | solution.py:361
  2663.8 1653.9 %reduce-scatter.28.cloned.1.call-start = ((), (), s32[]{:S(2)}) async-start(), calls=%async_computation.29 | async-start | bytes 31457280 | tf_op jit(solution)/shard_map/reduce_scatter | solution.py:355
  2677.2 1960.1 %all-reduce.12.cloned.1.call-start = ((), (), s32[]{:S(2)}) async-start(), calls=%async_computation.32 | async-start | bytes 50331648 | tf_op jit(solution)/shard_map/psum | solution.py:378
  (118 other events, 10836.6 us)
Sparse Core Ops, SparseCore 0:
  9.6 83.6 all-gather.16
  94.9 79.2 all-gather.12
  175.8 277.5 all-gather.20
  456.0 309.2 all-gather.18
  767.9 302.8 all-gather.14
  1073.4 38.9 all-gather.30
  1115.2 38.9 all-gather.28
  1155.7 148.3 all-gather.22
  1305.7 423.3 all-gather.24
  1730.6 423.3 all-gather.26
  2345.4 62.1 reduce-scatter.17
  2411.8 62.8 reduce-scatter.13
  2478.7 62.7 reduce-scatter.15
  2545.7 62.8 reduce-scatter.11
  2611.4 75.6 reduce-scatter.23
  2689.9 77.2 reduce-scatter.21
  2770.0 144.9 reduce-scatter.25
  2917.8 145.1 reduce-scatter.19
  3065.4 415.0 reduce-scatter.31
  3482.9 416.1 reduce-scatter.29
  3901.4 416.1 reduce-scatter.27
  4323.5 313.7 all-reduce.11
